TPU v7x, 32 devices: a whole 2x2x4 slice. The times are simulated.
32 devices in a mesh: frames: 2 (over x), date: 8 (over z, y), row: 2 (over core).
Axes of the slice: x: 2, y: 2, z: 4, core: 2. Of those that a mesh axis runs over, the one named last changes fastest.
Arguments:
- intensity: float32 [128, 512, 512], P(('frames', 'date'), 'row'), parts along dimension 0, may hold values from 0.05 to 20
Outputs:
- filtered: float32 [128, 512, 512], P(('frames', 'date'), 'row'), parts along dimension 0
- change: float32 [128, 512, 512], P(('frames', 'date'), 'row'), parts along dimension 0
There are 2 independent parts, one for each index of `frames`. A program takes and returns all parts, laid end to end along the dimension named above; each array names one. Nothing has to cross between parts.
All inputs are finite; a program needn't handle non-finite values.
Results may differ from a plain program's by a relative error of at most 0.00002.
Values sent between devices are 32-bit elements; how exact they have to be, the bound alone decides.
A program may use at most 64 MiB of HBM per device.

v0:
```python
import jax
import jax.numpy as jnp
from jax import lax
from jax.sharding import PartitionSpec as P

RADIUS = 3


def padded_2(cells, sides, width):
    for axis, dim in sides:
        count = lax.axis_size(axis)
        ends = count - 1
        head = lax.slice_in_dim(cells, 0, width, axis=dim)
        tail = lax.slice_in_dim(cells, cells.shape[dim] - width, cells.shape[dim], axis=dim)
        cells = jnp.concatenate(
            [
                lax.ppermute(tail, axis, [(i, (i + 1) % count) for i in range(ends)]),
                cells,
                lax.ppermute(head, axis, [((i + 1) % count, i) for i in range(ends)]),
            ],
            axis=dim,
        )
    return cells


def shifted(block, axis, distance):
    devices = range(lax.axis_size(axis))
    route = [(i - distance, i) for i in devices if i - distance in devices]
    return lax.ppermute(block, axis, route)


def rim_sum(haloed, rows_n):
    width = 2 * RADIUS + 1
    cols_n = haloed.shape[2]
    padded = jnp.pad(haloed, ((0, 0), (0, 0), (RADIUS, RADIUS)))
    across = padded[:, 0:rows_n, :]
    for offset in range(1, width):
        across = across + padded[:, offset : offset + rows_n, :]
    total = across[:, :, 0:cols_n]
    for offset in range(1, width):
        total = total + across[:, :, offset : offset + cols_n]
    return total


def valid_count(first, length, extent):
    places = first + jnp.arange(length, dtype=jnp.int32)
    counted = jnp.zeros((length,), jnp.float32)
    for offset in range(-RADIUS, RADIUS + 1):
        inside = (places + offset >= 0) & (places + offset < extent)
        counted = counted + inside.astype(jnp.float32)
    return counted


def on_device(intensity):
    rows_n = intensity.shape[1]
    cols_n = intensity.shape[2]
    row_groups = lax.axis_size("row")
    date_groups = lax.axis_size("date")
    total_dates = intensity.shape[0] * date_groups
    row_first = lax.axis_index("row") * rows_n
    row_count = valid_count(row_first, rows_n, rows_n * row_groups)
    col_count = valid_count(jnp.int32(0), cols_n, cols_n)
    count = row_count[:, None] * col_count[None, :]
    haloed = padded_2(intensity, (("row", 1),), RADIUS)
    local_mean = rim_sum(haloed, rows_n) / count[None]
    is_last = lax.axis_index("date") == date_groups - 1
    ratio_sum = lax.psum(jnp.sum(intensity / local_mean, axis=0), "date")
    scale = ratio_sum[None] / jnp.float32(total_dates)
    filtered = local_mean * scale
    following = shifted(haloed[0:1], "date", -1)
    follow_mean = rim_sum(following, rows_n) / count[None]
    successor = jnp.where(is_last, filtered[-1:], follow_mean * scale)
    logged = jnp.log(filtered)
    ahead = jnp.concatenate([logged[1:], jnp.log(successor)], axis=0)
    change = ahead - logged
    return (filtered, change)


def solution(mesh):
    return jax.shard_map(
        on_device,
        mesh=mesh,
        in_specs=(P(("frames", "date"), "row", None),),
        out_specs=(P(("frames", "date"), "row", None), P(("frames", "date"), "row", None)),
        check_vma=False,
    )
```

profile of v0, /device:TPU:0, one launch (start us, length us, event | category | flops | bytes accessed | tf_op | source)
XLA Modules:
  0.0 132.5 jit_solution(6093644278905989527)
XLA Ops:
  7.2 0.0 all-reduce.4.cloned.1.call-start
  7.2 1.0 fusion.42
  8.2 2.4 %collective-permute-start = (f32[8,3,512]{2,1,0:T(4,128)S(1)}, f32[8,3,512]{2,1,0:T(4,128)S(1)}, u32[]{:S(2)}, u32[]{:S(2)}) collective-permute-start(f32[8,3,512]{2,1,0:T(4,128)S(1)} %get-tuple-element.6), channel_id=1, source_target_pairs={{0,1},{2,3},{4,5},{6,7},{8,9},{10,11},{12,13},{14,15},{16,17},{18,... | collective-permute-start | bytes 147464 | tf_op jit(solution)/shard_map/ppermute | solution.py:17
  10.6 1.3 collective-permute-start.1
  12.0 0.1 broadcast_multiply_fusion.1
  12.1 0.0 collective-permute-done
  12.1 1.7 %collective-permute-done.1 = f32[8,3,512]{2,1,0:T(4,128)S(1)} collective-permute-done((f32[8,3,512]{2,1,0:T(4,128)S(1)}, f32[8,3,512]{2,1,0:T(4,128)S(1)}, u32[]{:S(2)}, u32[]{:S(2)}) %collective-permute-start.1) | collective-permute-done | bytes 49184 | tf_op jit(solution)/shard_map/ppermute | solution.py:19
  13.8 2.8 %pad_maximum_fusion = f32[8,262,512]{2,1,0:T(8,128)S(1)} fusion(f32[8,3,512]{2,1,0:T(4,128)S(1)} %collective-permute-done.1, f32[8,256,512]{2,1,0:T(8,128)} %param.1, f32[8,3,512]{2,1,0:T(4,128)S(1)} %collective-permute-done), kind=kLoop, calls=%fused_computation.13 | loop fusion | flops 2146304 | bytes 8585216 | tf_op jit(solution)/shard_map/concatenate | solution.py:15
  16.5 11.3 %fusion.5 = f32[8,256,518]{2,1,0:T(8,128)S(1)} fusion(f32[8,262,512]{2,1,0:T(8,128)S(1)} %pad_maximum_fusion), kind=kLoop, calls=%fused_computation.12 | loop fusion | flops 6365184 | bytes 8536064 | tf_op jit(solution)/shard_map/add | solution.py:38
  27.9 10.4 %fusion.6 = (f32[256,512]{1,0:T(8,128)}, f32[8,256,512]{2,1,0:T(8,128)}) fusion(f32[8,256,512]{2,1,0:T(8,128)} %param.1, f32[256,512]{1,0:T(8,128)S(1)} %broadcast_multiply_fusion.1, f32[8,256,518]{2,1,0:T(8,128)S(1)} %fusion.5), kind=kLoop, calls=%fused_computation.23 | loop fusion | flops 9306112 | bytes 38797312 | tf_op jit(solution)/shard_map/reduce_sum | solution.py:67
  38.3 0.0 all-reduce.4.cloned.1.call-update
  38.3 1.1 slice.141
  39.4 1.5 %collective-permute-start.2 = (f32[1,262,512]{2,1,0:T(8,128)S(1)}, f32[1,262,512]{2,1,0:T(8,128)S(1)}, u32[]{:S(2)}, u32[]{:S(2)}) collective-permute-start(f32[1,262,512]{2,1,0:T(8,128)S(1)} %slice.141), channel_id=1, source_target_pairs={{2,0},{4,2},{6,4},{8,6},{10,8},{12,10},{14,12},{3,1},{5,3},{7,5},{... | collective-permute-start | bytes 1609736 | tf_op jit(solution)/shard_map/ppermute | solution.py:29
  40.9 74.4 %all-reduce.4.cloned.1.call-done = f32[256,512]{1,0:T(8,128)} async-done(((f32[256,512]{1,0:T(8,128)}), f32[256,512]{1,0:T(8,128)}) %all-reduce.4.cloned.1.call-update) | async-done | bytes 524304 | tf_op jit(solution)/shard_map/psum | solution.py:67
  115.3 1.1 broadcast_multiply_fusion
  116.4 3.3 %fusion.41 = (f32[8,256,512]{2,1,0:T(8,128)S(1)}, f32[8,256,512]{2,1,0:T(8,128)S(1)}) fusion(f32[256,512]{1,0:T(8,128)S(1)} %broadcast_multiply_fusion, f32[8,256,512]{2,1,0:T(8,128)} %get-tuple-element.5, f32[256,512]{1,0:T(8,128)S(1)} %broadcast_multiply_fusion.1), kind=kLoop, calls=%fused_computation.88 | loop fusion | flops 2097152 | bytes 13631488 | tf_op jit(solution)/shard_map/log | solution.py:73
  119.7 0.0 copy-start.1
  119.7 0.0 copy-start.2
  119.7 0.5 slice.139
  120.3 0.0 collective-permute-done.2
  120.3 1.4 %fusion.12 = f32[1,256,518]{2,1,0:T(8,128)S(1)} fusion(f32[1,262,512]{2,1,0:T(8,128)S(1)} %collective-permute-done.2), kind=kLoop, calls=%fused_computation.36 | loop fusion | flops 795648 | bytes 1067008 | tf_op jit(solution)/shard_map/add | solution.py:38
  121.7 0.0 copy-done.2
  121.7 0.9 fusion.16
  122.6 3.0 %maximum_subtract_fusion = f32[8,256,512]{2,1,0:T(8,128)} fusion(f32[1,256,512]{2,1,0:T(8,128)S(1)} %fusion.16, f32[7,256,512]{2,1,0:T(8,128)S(1)} %slice.139, f32[8,256,512]{2,1,0:T(8,128)S(1)} %get-tuple-element.3), kind=kLoop, calls=%fused_computation.20 | loop fusion | flops 2097152 | bytes 12582912 | tf_op jit(solution)/shard_map/sub | solution.py:75
  (5 shorter events, 0.0 us)
Async XLA Ops:
  7.2 108.1 %all-reduce.4.cloned.1.call-start = ((), (), s32[]{:S(2)}) async-start(), calls=%async_computation | async-start | bytes 1048576 | tf_op jit(solution)/shard_map/psum | solution.py:67
  8.2 3.9 %collective-permute-start = (f32[8,3,512]{2,1,0:T(4,128)S(1)}, f32[8,3,512]{2,1,0:T(4,128)S(1)}, u32[]{:S(2)}, u32[]{:S(2)}) collective-permute-start(f32[8,3,512]{2,1,0:T(4,128)S(1)} %get-tuple-element.6), channel_id=1, source_target_pairs={{0,1},{2,3},{4,5},{6,7},{8,9},{10,11},{12,13},{14,15},{16,17},{18,... | collective-permute-start | bytes 147464 | tf_op jit(solution)/shard_map/ppermute | solution.py:17
  10.6 3.1 %collective-permute-start.1 = (f32[8,3,512]{2,1,0:T(4,128)S(1)}, f32[8,3,512]{2,1,0:T(4,128)S(1)}, u32[]{:S(2)}, u32[]{:S(2)}) collective-permute-start(f32[8,3,512]{2,1,0:T(4,128)S(1)} %get-tuple-element.7), channel_id=1, source_target_pairs={{1,0},{3,2},{5,4},{7,6},{9,8},{11,10},{13,12},{15,14},{17,16},{19,... | collective-permute-start | bytes 147464 | tf_op jit(solution)/shard_map/ppermute | solution.py:19
  16.5 11.3 %copy-start = (f32[8,262,512]{2,1,0:T(8,128)}, f32[8,262,512]{2,1,0:T(8,128)S(1)}, u32[]{:S(2)}) copy-start(f32[8,262,512]{2,1,0:T(8,128)S(1)} %pad_maximum_fusion) | copy-start | bytes 12877828
  39.4 80.9 %collective-permute-start.2 = (f32[1,262,512]{2,1,0:T(8,128)S(1)}, f32[1,262,512]{2,1,0:T(8,128)S(1)}, u32[]{:S(2)}, u32[]{:S(2)}) collective-permute-start(f32[1,262,512]{2,1,0:T(8,128)S(1)} %slice.141), channel_id=1, source_target_pairs={{2,0},{4,2},{6,4},{8,6},{10,8},{12,10},{14,12},{3,1},{5,3},{7,5},{... | collective-permute-start | bytes 1609736 | tf_op jit(solution)/shard_map/ppermute | solution.py:29
  119.7 3.0 %copy-start.1 = (f32[8,256,512]{2,1,0:T(8,128)}, f32[8,256,512]{2,1,0:T(8,128)S(1)}, u32[]{:S(2)}) copy-start(f32[8,256,512]{2,1,0:T(8,128)S(1)} %get-tuple-element.3) | copy-start | bytes 12582916
  119.7 2.0 %copy-start.2 = (f32[256,512]{1,0:T(8,128)S(1)}, f32[256,512]{1,0:T(8,128)}, u32[]{:S(2)}) copy-start(f32[256,512]{1,0:T(8,128)} %all-reduce.4.cloned.1.call-done) | copy-start | bytes 1572868
Sparse Core Ops, SparseCore 0:
  38.4 76.8 all-reduce.3
where the time goes:
time: 133 us
  waiting for transfers between devices  76.1 us (57%)
  other arithmetic  34.4 us (26%)
  between operations  14.2 us (11%)
  starting transfers between devices  5.2 us (4%)
  local copies, waits for them, and re-layouts  2.64 us (2%)
    psum x1, waiting for transfers between devices, on_device(): ratio_sum = lax.psum(jnp.sum(intensity / local_mean, axis=0), 'date')  74.4 us
    add x2, other arithmetic, rim_sum(): across = across + padded[:, offset:offset + rows_n, :]  12.7 us
    reduce_sum x1, other arithmetic, on_device(): ratio_sum = lax.psum(jnp.sum(intensity / local_mean, axis=0), 'date')  10.4 us
    log x1, other arithmetic, on_device(): logged = jnp.log(filtered)  3.32 us
    sub x1, other arithmetic, on_device(): change = ahead - logged  3.05 us
    concatenate x1, other arithmetic, padded_2(): jnp.concatenate([lax.ppermute(tail, axis, [(i, (i + 1) % count) for i in...  2.75 us
  transfers between devices with their start and end apart: 4, of which 2 were waited for; matrix products, arithmetic and copies ran while one was open for 5% of the time, Pallas kernels for 0%

commit v1 on v0

--- a/solution.py
+++ b/solution.py
@@ -64,7 +64,7 @@
     haloed = padded_2(intensity, (("row", 1),), RADIUS)
     local_mean = rim_sum(haloed, rows_n) / count[None]
     is_last = lax.axis_index("date") == date_groups - 1
-    ratio_sum = lax.psum(jnp.sum(intensity / local_mean, axis=0), "date")
+    ratio_sum = jnp.sum(lax.all_gather(jnp.sum(intensity / local_mean, axis=0), "date"), axis=0)
     scale = ratio_sum[None] / jnp.float32(total_dates)
     filtered = local_mean * scale
     following = shifted(haloed[0:1], "date", -1)

time: 133 us -> 137 us (1.030)
  waiting for transfers between devices: 76.1 us -> 77.7 us
  other arithmetic: 34.4 us -> 36 us
    psum x1 -> x0, waiting for transfers between devices: 74.4 us -> none  [on_device(): ratio_sum = lax.psum(jnp.sum(intensity / local_mean, axis=0), 'date')]
    all_gather x0 -> x1, waiting for transfers between devices: none -> 55.1 us  [on_device(): lax.all_gather(jnp.sum(intensity / local_mean, axis=0), 'date')]
    ppermute x1, waiting for transfers between devices: 0.01 us -> 20.9 us  [shifted(): return lax.ppermute(block, axis, route)]
    reduce_sum x1 -> x2, other arithmetic: 10.4 us -> 13.1 us  [the longest x1 10.4 us: on_device(): jnp.sum(intensity / local_mean, axis=0)]
  transfers between devices with their start and end apart: 4 -> 4, of which waited for: 2 -> 3; matrix products, arithmetic and copies ran while one was open for 5% -> 2% of each run, Pallas kernels for 0% -> 0%
where the time goes in v1:
time: 137 us
  waiting for transfers between devices  77.7 us (57%)
  other arithmetic  36 us (26%)
  between operations  14.2 us (10%)
  starting transfers between devices  5.2 us (4%)
  local copies, waits for them, and re-layouts  3.75 us (3%)
    all_gather x1, waiting for transfers between devices, on_device(): lax.all_gather(jnp.sum(intensity / local_mean, axis=0), 'date')  55.1 us
    ppermute x1, waiting for transfers between devices, shifted(): return lax.ppermute(block, axis, route)  20.9 us
    add x2, other arithmetic, rim_sum(): across = across + padded[:, offset:offset + rows_n, :]  12.7 us
    reduce_sum x1, other arithmetic, on_device(): jnp.sum(intensity / local_mean, axis=0)  10.4 us
    log x1, other arithmetic, on_device(): logged = jnp.log(filtered)  3.32 us
    sub x1, other arithmetic, on_device(): change = ahead - logged  3.04 us
    concatenate x1, other arithmetic, padded_2(): jnp.concatenate([lax.ppermute(tail, axis, [(i, (i + 1) % count) for i in...  2.75 us
  transfers between devices with their start and end apart: 4, of which 3 were waited for; matrix products, arithmetic and copies ran while one was open for 2% of the time, Pallas kernels for 0%

profile of v1, /device:TPU:0, one launch (start us, length us, event | category | flops | bytes accessed | tf_op | source)
XLA Modules:
  0.0 136.9 jit_solution(7975592479261989748)
XLA Ops:
  7.2 0.0 all-gather.3.cloned.1.call-start
  7.2 1.0 fusion.42
  8.2 2.4 %collective-permute-start = (f32[8,3,512]{2,1,0:T(4,128)S(1)}, f32[8,3,512]{2,1,0:T(4,128)S(1)}, u32[]{:S(2)}, u32[]{:S(2)}) collective-permute-start(f32[8,3,512]{2,1,0:T(4,128)S(1)} %get-tuple-element.6), channel_id=1, source_target_pairs={{0,1},{2,3},{4,5},{6,7},{8,9},{10,11},{12,13},{14,15},{16,17},{18,... | collective-permute-start | bytes 147464 | tf_op jit(solution)/shard_map/ppermute | solution.py:17
  10.6 1.3 collective-permute-start.1
  12.0 0.1 broadcast_multiply_fusion.1
  12.1 0.0 collective-permute-done
  12.1 1.7 %collective-permute-done.1 = f32[8,3,512]{2,1,0:T(4,128)S(1)} collective-permute-done((f32[8,3,512]{2,1,0:T(4,128)S(1)}, f32[8,3,512]{2,1,0:T(4,128)S(1)}, u32[]{:S(2)}, u32[]{:S(2)}) %collective-permute-start.1) | collective-permute-done | bytes 49184 | tf_op jit(solution)/shard_map/ppermute | solution.py:19
  13.8 2.8 %pad_maximum_fusion = f32[8,262,512]{2,1,0:T(8,128)S(1)} fusion(f32[8,3,512]{2,1,0:T(4,128)S(1)} %collective-permute-done.1, f32[8,256,512]{2,1,0:T(8,128)} %param.1, f32[8,3,512]{2,1,0:T(4,128)S(1)} %collective-permute-done), kind=kLoop, calls=%fused_computation.13 | loop fusion | flops 2146304 | bytes 8585216 | tf_op jit(solution)/shard_map/concatenate | solution.py:15
  16.5 11.3 %fusion.5 = f32[8,256,518]{2,1,0:T(8,128)S(1)} fusion(f32[8,262,512]{2,1,0:T(8,128)S(1)} %pad_maximum_fusion), kind=kLoop, calls=%fused_computation.12 | loop fusion | flops 6365184 | bytes 8536064 | tf_op jit(solution)/shard_map/add | solution.py:38
  27.9 10.4 %fusion.6 = (f32[256,512]{1,0:T(8,128)}, f32[8,256,512]{2,1,0:T(8,128)}) fusion(f32[8,256,512]{2,1,0:T(8,128)} %param.1, f32[256,512]{1,0:T(8,128)S(1)} %broadcast_multiply_fusion.1, f32[8,256,518]{2,1,0:T(8,128)S(1)} %fusion.5), kind=kLoop, calls=%fused_computation.23 | loop fusion | flops 9306112 | bytes 38797312 | tf_op jit(solution)/shard_map/reduce_sum | solution.py:67
  38.3 0.0 all-gather.3.cloned.1.call-update
  38.3 1.1 slice.141
  39.4 0.6 copy.3
  39.9 1.5 %collective-permute-start.2 = (f32[1,262,512]{2,0,1:T(1,128)S(1)}, f32[1,262,512]{2,0,1:T(1,128)S(1)}, u32[]{:S(2)}, u32[]{:S(2)}) collective-permute-start(f32[1,262,512]{2,0,1:T(1,128)S(1)} %copy.3), channel_id=1, source_target_pairs={{2,0},{4,2},{6,4},{8,6},{10,8},{12,10},{14,12},{3,1},{5,3},{7,5},{... | collective-permute-start | bytes 1609736 | tf_op jit(solution)/shard_map/ppermute | solution.py:29
  41.4 20.9 %collective-permute-done.2 = f32[1,262,512]{2,0,1:T(1,128)S(1)} collective-permute-done((f32[1,262,512]{2,0,1:T(1,128)S(1)}, f32[1,262,512]{2,0,1:T(1,128)S(1)}, u32[]{:S(2)}, u32[]{:S(2)}) %collective-permute-start.2) | collective-permute-done | bytes 536608 | tf_op jit(solution)/shard_map/ppermute | solution.py:29
  62.3 1.4 %fusion.12 = f32[1,256,518]{2,1,0:T(8,128)S(1)} fusion(f32[1,262,512]{2,1,0:T(8,128)S(1)} %copy.4), kind=kLoop, calls=%fused_computation.36 | loop fusion | flops 795648 | bytes 1067008 | tf_op jit(solution)/shard_map/add | solution.py:38
  63.8 55.1 %all-gather.3.cloned.1.call-done = f32[2048,512]{1,0:T(8,128)} async-done(((f32[256,512]{1,0:T(8,128)}), f32[2048,512]{1,0:T(8,128)}) %all-gather.3.cloned.1.call-update) | async-done | bytes 4194320 | tf_op jit(solution)/shard_map/all_gather | solution.py:67
  118.9 2.7 %reduce_sum.19 = f32[256,512]{1,0:T(8,128)S(1)} reduce(f32[8,256,512]{2,1,0:T(8,128)} %bitcast.3, f32[]{:T(128)} %constant.14.clone.1), dimensions={0}, to_apply=%region_1.2 | reduce | flops 917504 | bytes 4718596 | tf_op jit(solution)/shard_map/reduce_sum | solution.py:67
  121.6 3.3 %fusion.41 = (f32[8,256,512]{2,1,0:T(8,128)S(1)}, f32[8,256,512]{2,1,0:T(8,128)S(1)}) fusion(f32[256,512]{1,0:T(8,128)S(1)} %broadcast_multiply_fusion, f32[8,256,512]{2,1,0:T(8,128)} %get-tuple-element.5, f32[256,512]{1,0:T(8,128)S(1)} %broadcast_multiply_fusion.1), kind=kLoop, calls=%fused_computation.88 | loop fusion | flops 2097152 | bytes 13631488 | tf_op jit(solution)/shard_map/log | solution.py:73
  125.0 0.0 copy-start.1
  125.0 0.5 slice.139
  125.5 0.9 fusion.16
  126.5 0.5 copy-done.1
  127.0 3.0 %maximum_subtract_fusion = f32[8,256,512]{2,1,0:T(8,128)} fusion(f32[1,256,512]{2,1,0:T(8,128)S(1)} %fusion.16, f32[7,256,512]{2,1,0:T(8,128)S(1)} %slice.139, f32[8,256,512]{2,1,0:T(8,128)S(1)} %get-tuple-element.3), kind=kLoop, calls=%fused_computation.20 | loop fusion | flops 2097152 | bytes 12582912 | tf_op jit(solution)/shard_map/sub | solution.py:75
  (6 shorter events, 0.1 us)
Async XLA Ops:
  7.2 111.7 %all-gather.3.cloned.1.call-start = ((), (), s32[]{:S(2)}) async-start(), calls=%async_computation | async-start | bytes 4718592 | tf_op jit(solution)/shard_map/all_gather | solution.py:67
  8.2 3.9 %collective-permute-start = (f32[8,3,512]{2,1,0:T(4,128)S(1)}, f32[8,3,512]{2,1,0:T(4,128)S(1)}, u32[]{:S(2)}, u32[]{:S(2)}) collective-permute-start(f32[8,3,512]{2,1,0:T(4,128)S(1)} %get-tuple-element.6), channel_id=1, source_target_pairs={{0,1},{2,3},{4,5},{6,7},{8,9},{10,11},{12,13},{14,15},{16,17},{18,... | collective-permute-start | bytes 147464 | tf_op jit(solution)/shard_map/ppermute | solution.py:17
  10.6 3.1 %collective-permute-start.1 = (f32[8,3,512]{2,1,0:T(4,128)S(1)}, f32[8,3,512]{2,1,0:T(4,128)S(1)}, u32[]{:S(2)}, u32[]{:S(2)}) collective-permute-start(f32[8,3,512]{2,1,0:T(4,128)S(1)} %get-tuple-element.7), channel_id=1, source_target_pairs={{1,0},{3,2},{5,4},{7,6},{9,8},{11,10},{13,12},{15,14},{17,16},{19,... | collective-permute-start | bytes 147464 | tf_op jit(solution)/shard_map/ppermute | solution.py:19
  16.5 11.3 %copy-start = (f32[8,262,512]{2,1,0:T(8,128)}, f32[8,262,512]{2,1,0:T(8,128)S(1)}, u32[]{:S(2)}) copy-start(f32[8,262,512]{2,1,0:T(8,128)S(1)} %pad_maximum_fusion) | copy-start | bytes 12877828
  39.9 22.4 %collective-permute-start.2 = (f32[1,262,512]{2,0,1:T(1,128)S(1)}, f32[1,262,512]{2,0,1:T(1,128)S(1)}, u32[]{:S(2)}, u32[]{:S(2)}) collective-permute-start(f32[1,262,512]{2,0,1:T(1,128)S(1)} %copy.3), channel_id=1, source_target_pairs={{2,0},{4,2},{6,4},{8,6},{10,8},{12,10},{14,12},{3,1},{5,3},{7,5},{... | collective-permute-start | bytes 1609736 | tf_op jit(solution)/shard_map/ppermute | solution.py:29
  125.0 2.0 %copy-start.1 = (f32[8,256,512]{2,1,0:T(8,128)}, f32[8,256,512]{2,1,0:T(8,128)S(1)}, u32[]{:S(2)}) copy-start(f32[8,256,512]{2,1,0:T(8,128)S(1)} %get-tuple-element.3) | copy-start | bytes 12582916
Sparse Core Ops, SparseCore 0:
  38.4 80.4 all-gather.2
